TPU v7x, 32 devices: a whole 2x2x4 slice. The times are simulated.
32 devices in a mesh: row: 4 (over z), col: 8 (over y, x, core).
Axes of the slice: x: 2, y: 2, z: 4, core: 2. Of those that a mesh axis runs over, the one named last changes fastest.
Arguments:
- diag_inverse: float32 [1024, 1024], P(('row', 'col')), as said below
- row_basis: float32 [16, 128, 1024], P('row', 'col'), may hold values from -6 to 6
- row_coef: float32 [16, 128, 1024], P('row', 'col'), may hold values from -0.09375 to 0.09375
- row_ranks: int32 [16], P('row'), may hold values from 16 to 128, as said below
- col_basis: float32 [24, 128, 1024], P('col', 'row'), may hold values from -6 to 6
- col_coef: float32 [24, 128, 1024], P('col', 'row'), may hold values from -0.09375 to 0.09375
- col_ranks: int32 [24], P('col'), may hold values from 16 to 128, as said below
- tile_basis: float32 [16, 24, 1024, 128], P('row', 'col'), may hold values from -6 to 6
- tile_coef: float32 [16, 24, 1024, 128], P('row', 'col'), may hold values from -0.5 to 0.5
- tile_ranks: int32 [16, 24], P('row', 'col'), may hold values from 16 to 128, as said below
Outputs:
- new_basis: bfloat16 [16, 24, 1024, 128], P('row', 'col')
- new_coef: bfloat16 [16, 24, 1024, 128], P('row', 'col')
Inputs may be any that keep to these rules, and one draw needn't show every extreme that they name: `row_ranks`: rank of each panel tile; the smallest and largest values occur in every draw. `col_ranks`: rank of each panel tile; the smallest and largest values occur in every draw. `tile_ranks`: rank of each trailing tile; the smallest and largest values occur in every draw. `diag_inverse`: lower triangular with a positive diagonal.
All inputs are finite; a program needn't handle non-finite values.
Results may differ from a plain program's by a relative error of at most 0.001.
Values sent between devices are 32-bit elements; how exact they have to be, the bound alone decides.
A program may use at most 128 MiB of HBM per device.

v0:
```python
import math

import jax
import jax.numpy as jnp
from jax import lax
from jax.sharding import PartitionSpec as P

HIGHEST = lax.Precision.HIGHEST


def small_inverse(gram_matrix, eye_block):
    factor = jnp.linalg.cholesky(gram_matrix)
    return jax.scipy.linalg.solve_triangular(factor, eye_block, lower=True)


def orthonormal_twice(sketch_block, rank_keep):
    rank_width = rank_keep.shape[-1]
    eye_one = jnp.eye(rank_width, dtype=jnp.float32)[None, :, :]
    eye_block = jnp.broadcast_to(eye_one, (sketch_block.shape[0], rank_width, rank_width))
    gram_matrix = jnp.einsum("tnr,tns->trs", sketch_block, sketch_block, precision=HIGHEST)
    gram_matrix = gram_matrix + eye_one * (1.0 - rank_keep)[:, None, :]
    first_inverse = small_inverse(gram_matrix, eye_block)
    half_gram = jnp.einsum("trs,tus->tru", gram_matrix, first_inverse, precision=HIGHEST)
    second_gram = jnp.einsum("trs,tsu->tru", first_inverse, half_gram, precision=HIGHEST)
    second_gram = 0.5 * (second_gram + jnp.swapaxes(second_gram, 1, 2))
    second_inverse = small_inverse(second_gram, eye_block)
    combined = jnp.einsum("trs,tsu->tru", second_inverse, first_inverse, precision=HIGHEST)
    return jnp.einsum("tnr,tsr->tns", sketch_block, combined, precision=HIGHEST)


def share_mask(panel_ranks, rank_share, position):
    columns = position * rank_share + jnp.arange(rank_share, dtype=jnp.int32)
    return (columns[None, :] < panel_ranks[:, None]).astype(jnp.float32)[:, :, None]


def solve_rows(inverse_factor, coef_rows):
    tile_count, rank_rows, order = coef_rows.shape
    flat_rows = coef_rows.reshape(tile_count * rank_rows, order)
    solved = jnp.dot(flat_rows, inverse_factor.T, precision=HIGHEST)
    return solved.reshape(tile_count, rank_rows, order)


def body(
    diag_inverse,
    row_basis,
    row_coef,
    row_ranks,
    col_basis,
    col_coef,
    col_ranks,
    tile_basis,
    tile_coef,
    tile_ranks,
):
    inverse_whole = lax.all_gather(diag_inverse, ("row", "col"), axis=0, tiled=True)
    row_keep = share_mask(row_ranks, row_basis.shape[1], lax.axis_index("col"))
    row_left = row_basis * row_keep
    row_send = row_coef * row_keep
    row_send = solve_rows(inverse_whole, row_send)
    row_left, row_solved = (
        lax.all_gather(row_left, "col", axis=1, tiled=True),
        lax.all_gather(row_send, "col", axis=1, tiled=True),
    )
    col_keep = share_mask(col_ranks, col_basis.shape[1], lax.axis_index("row"))
    col_left = col_basis * col_keep
    col_send = col_coef * col_keep
    col_send = solve_rows(inverse_whole, col_send)
    col_left, col_solved = (
        lax.all_gather(col_left, "row", axis=1, tiled=True),
        lax.all_gather(col_send, "row", axis=1, tiled=True),
    )
    local_rows, local_cols, order, rank_width = tile_basis.shape
    all_coupling = jnp.dot(
        row_solved.reshape(local_rows * rank_width, order),
        col_solved.reshape(local_cols * rank_width, order).T,
        precision=HIGHEST,
    )
    coupling = jnp.transpose(
        all_coupling.reshape(local_rows, rank_width, local_cols, rank_width), (0, 2, 1, 3)
    )
    tile_count = local_rows * local_cols
    rank_keep = (
        jnp.arange(rank_width, dtype=jnp.int32)[None, None, :] < tile_ranks[:, :, None]
    ).astype(jnp.float32)
    masked_left = tile_basis * rank_keep[:, :, None, :]
    masked_right = tile_coef * rank_keep[:, :, None, :]

    def make_sketch(tile_left, tile_right, left_panel, pair_coupling, right_panel):
        inner_gram = jnp.dot(tile_right.T, tile_right, precision=HIGHEST)
        cross_term = jnp.dot(right_panel, tile_right, precision=HIGHEST)
        return jnp.dot(tile_left, inner_gram, precision=HIGHEST) - jnp.dot(
            left_panel.T, jnp.dot(pair_coupling, cross_term, precision=HIGHEST), precision=HIGHEST
        )

    sketch_inner = jax.vmap(make_sketch, in_axes=(0, 0, None, 0, 0))
    sketch = jax.vmap(sketch_inner, in_axes=(0, 0, 0, 0, None))(
        masked_left, masked_right, row_left, coupling, col_left
    )
    flat_keep = rank_keep.reshape(tile_count, rank_width)
    flat_sketch = sketch.reshape(tile_count, order, rank_width)
    ortho_basis = orthonormal_twice(flat_sketch, flat_keep).reshape(
        local_rows, local_cols, order, rank_width
    )

    def make_coef(tile_left, tile_right, left_panel, pair_coupling, right_panel, basis_block):
        first_part = jnp.dot(
            tile_right, jnp.dot(tile_left.T, basis_block, precision=HIGHEST), precision=HIGHEST
        )
        left_proj = jnp.dot(left_panel, basis_block, precision=HIGHEST)
        second_part = jnp.dot(
            right_panel.T, jnp.dot(pair_coupling.T, left_proj, precision=HIGHEST), precision=HIGHEST
        )
        return first_part - second_part

    coef_inner = jax.vmap(make_coef, in_axes=(0, 0, None, 0, 0, 0))
    new_coef = jax.vmap(coef_inner, in_axes=(0, 0, 0, 0, None, 0))(
        masked_left, masked_right, row_left, coupling, col_left, ortho_basis
    )
    scaled_basis = ortho_basis * math.sqrt(order)
    return (scaled_basis.astype(jnp.bfloat16), new_coef.astype(jnp.bfloat16))


def solution(mesh):
    placed = (
        P(("row", "col"), None),
        P("row", "col", None),
        P("row", "col", None),
        P("row"),
        P("col", "row", None),
        P("col", "row", None),
        P("col"),
        P("row", "col", None, None),
        P("row", "col", None, None),
        P("row", "col"),
    )
    return jax.shard_map(
        body,
        mesh=mesh,
        in_specs=placed,
        out_specs=(P("row", "col", None, None), P("row", "col", None, None)),
        check_vma=False,
    )
```

profile of v0, /device:TPU:0, one launch (start us, length us, event | category | flops | bytes accessed | tf_op | source)
XLA Modules:
  0.0 816.8 jit_solution(13552350333110011284)
XLA Ops:
  10.6 64.7 %all-gather.8.cloned.1.call-done = f32[1024,1024]{1,0:T(8,128)} async-done(((f32[32,1024]{1,0:T(8,128)}), f32[1024,1024]{1,0:T(8,128)}) %all-gather.8.cloned.1.call-update) | async-done | bytes 4194320 | tf_op jit(solution)/shard_map/all_gather | solution.py:55
  75.4 7.2 fusion.7
  82.7 7.2 fusion.9
  91.7 15.2 %fusion.47 = f32[4,3,128,128]{3,2,1,0:T(8,128)S(1)} fusion(f32[4,3,1024,128]{3,2,1,0:T(8,128)} %param.21, f32[4,3,128]{2,1,0:T(4,128)S(1)} %fusion.46), kind=kOutput, calls=%fused_computation.71 | convolution fusion | flops 2419064832 | bytes 7084032 | tf_op jit(solution)/shard_map/vmap(vmap())/dot_general | solution.py:89
  106.9 6.5 all-gather.14.cloned.1.call-done
  113.3 6.7 fusion.1
  120.1 31.3 %all-gather.12.cloned.1.call-done = f32[3,128,1024]{2,1,0:T(8,128)} async-done(((f32[3,32,1024]{2,1,0:T(8,128)}), f32[3,128,1024]{2,1,0:T(8,128)}) %all-gather.12.cloned.1.call-update) | async-done | bytes 1572880 | tf_op jit(solution)/shard_map/all_gather | solution.py:70
  151.4 28.4 %all-gather.10.cloned.1.call-done = f32[4,128,1024]{2,1,0:T(8,128)} async-done(((f32[4,16,1024]{2,1,0:T(8,128)}), f32[4,128,1024]{2,1,0:T(8,128)}) %all-gather.10.cloned.1.call-update) | async-done | bytes 2097168 | tf_op jit(solution)/shard_map/all_gather | solution.py:62
  179.8 5.5 fusion.15
  186.3 23.1 %all-gather.6.cloned.1.call-done = f32[4,128,1024]{2,1,0:T(8,128)} async-done(((f32[4,16,1024]{2,1,0:T(8,128)}), f32[4,128,1024]{2,1,0:T(8,128)}) %all-gather.6.cloned.1.call-update) | async-done | bytes 2097168 | tf_op jit(solution)/shard_map/all_gather | solution.py:61
  209.4 7.2 fusion.19
  216.6 8.5 %bitcast_subtract_fusion.1 = f32[4,3,1024,128]{3,2,1,0:T(8,128)S(1)} fusion(f32[4,1024,3,128]{3,1,2,0:T(8,128)S(1)} %fusion.19, f32[4,3,128,128]{3,2,1,0:T(8,128)S(1)} %fusion.47, f32[4,3,1024,128]{3,2,1,0:T(8,128)} %param.20, f32[4,3,128]{2,1,0:T(4,128)S(1)} %fusion.46), kind=kOutput, calls=%fused_computation.2 | convolution fusion | flops 2419064832 | bytes 19666944 | tf_op jit(solution)/shard_map/vmap(vmap())/dot_general | solution.py:91
  225.1 2.6 copy-done
  227.8 10.5 %convolution_add_fusion = f32[12,128,128]{1,2,0:T(8,128)S(1)} fusion(f32[12,1024,128]{2,1,0:T(8,128)S(1)} %bitcast.84, f32[12,128]{1,0:T(8,128)S(1)} %convert_subtract_fusion, f32[128,128]{0,1:T(8,128)S(1)} %fusion.45), kind=kOutput, calls=%fused_computation.27 | convolution fusion | flops 2416312320 | bytes 7149568 | tf_op jit(solution)/shard_map/tnr,tns->trs/dot_general | solution.py:20
  238.7 141.1 %custom-call.8 = f32[12,128,128]{2,1,0:T(8,128)S(1)} custom-call(f32[12,128,128]{2,1,0:T(8,128)S(1)} %fusion.33), custom_call_target="Cholesky" | custom-call | tf_op jit(solution)/shard_map/jit(cholesky)/cholesky | solution.py:12
  380.1 118.5 %custom-call.9 = f32[12,1,128,128]{2,3,1,0:T(8,128)} custom-call(f32[12,1,128,128]{3,2,1,0:T(8,128)S(1)} %select_bitcast_fusion.1), custom_call_target="InvertDiagBlocksLowerTriangular" | custom-call | tf_op jit(solution)/shard_map/jit(_solve_triangular)/vmap()/triangular_solve | solution.py:13
  498.6 2.5 fusion.31
  507.1 141.6 %custom-call.10 = f32[12,128,128]{2,1,0:T(8,128)S(1)} custom-call(f32[12,128,128]{2,1,0:T(8,128)} %fusion.29), custom_call_target="Cholesky" | custom-call | tf_op jit(solution)/shard_map/jit(cholesky)/cholesky | solution.py:12
  649.1 117.9 %custom-call.11 = f32[12,1,128,128]{2,3,1,0:T(8,128)S(1)} custom-call(f32[12,1,128,128]{3,2,1,0:T(8,128)S(1)} %select_bitcast_fusion), custom_call_target="InvertDiagBlocksLowerTriangular" | custom-call | tf_op jit(solution)/shard_map/jit(_solve_triangular)/vmap()/triangular_solve | solution.py:13
  769.3 8.5 %fusion.51 = f32[12,1024,128]{2,1,0:T(8,128)S(1)} fusion(f32[12,1024,128]{2,1,0:T(8,128)} %bitcast.85, f32[12,128,128]{2,1,0:T(8,128)S(1)} %fusion.50), kind=kOutput, calls=%fused_computation.75 | convolution fusion | flops 2415919104 | bytes 13369344 | tf_op jit(solution)/shard_map/tnr,tsr->tns/dot_general | solution.py:28
  777.9 10.4 %fusion.3 = f32[4,3,128,128]{3,2,1,0:T(8,128)S(1)} fusion(f32[4,3,1024,128]{3,2,1,0:T(8,128)S(1)} %bitcast.86, f32[4,3,1024,128]{3,2,1,0:T(8,128)S(1)} %bitcast.90, f32[4,3,128]{2,1,0:T(4,128)S(1)} %fusion.46), kind=kOutput, calls=%fused_computation.6 | convolution fusion | flops 2417491968 | bytes 13375488 | tf_op jit(solution)/shard_map/vmap(vmap())/dot_general | solution.py:107
  790.6 4.8 fusion.17
  796.9 5.4 fusion.22
  802.3 7.8 fusion
  (64 shorter events, 19.3 us)
Async XLA Ops:
  7.2 75.5 %copy-start.6 = (s32[4]{0:T(128)S(1)}, s32[4]{0:T(128)}, u32[]{:S(2)}) copy-start(s32[4]{0:T(128)} %param.16) | copy-start | bytes 52
  7.2 75.6 %copy-start.3 = (f32[4,16,1024]{2,1,0:T(8,128)S(1)}, f32[4,16,1024]{2,1,0:T(8,128)}, u32[]{:S(2)}) copy-start(f32[4,16,1024]{2,1,0:T(8,128)} %param.15) | copy-start | bytes 786436
  7.2 83.3 %copy-start.4 = (f32[4,16,1024]{2,1,0:T(8,128)S(1)}, f32[4,16,1024]{2,1,0:T(8,128)}, u32[]{:S(2)}) copy-start(f32[4,16,1024]{2,1,0:T(8,128)} %param.14) | copy-start | bytes 786436
  7.2 84.2 %copy-start.5 = (s32[4,3]{1,0:T(4,128)S(1)}, s32[4,3]{1,0:T(4,128)}, u32[]{:S(2)}) copy-start(s32[4,3]{1,0:T(4,128)} %param.22) | copy-start | bytes 148
  7.2 68.1 %all-gather.8.cloned.1.call-start = ((), (), s32[]{:S(2)}) async-start(), calls=%async_computation.1 | async-start | bytes 4325376 | tf_op jit(solution)/shard_map/all_gather | solution.py:55
  7.9 105.4 %all-gather.14.cloned.1.call-start = ((), (), s32[]{:S(2)}) async-start(), calls=%async_computation.4 | async-start | bytes 1966080 | tf_op jit(solution)/shard_map/all_gather | solution.py:69
  10.6 140.8 %all-gather.12.cloned.1.call-start = ((), (), s32[]{:S(2)}) async-start(), calls=%async_computation.3 | async-start | bytes 1966080 | tf_op jit(solution)/shard_map/all_gather | solution.py:70
  82.6 97.3 %all-gather.10.cloned.1.call-start = ((), (), s32[]{:S(2)}) async-start(), calls=%async_computation.2 | async-start | bytes 2359296 | tf_op jit(solution)/shard_map/all_gather | solution.py:62
  90.0 119.5 %all-gather.6.cloned.1.call-start = ((), (), s32[]{:S(2)}) async-start(), calls=%async_computation | async-start | bytes 2359296 | tf_op jit(solution)/shard_map/all_gather | solution.py:61
  225.1 2.7 copy-start
  768.4 9.4 %slice-start.2 = ((s8[6291456]{0:T(1024)(128)(4,1)}), s8[4194304]{0:T(1024)(128)(4,1)S(1)}, s32[]{:S(2)}) async-start(s8[6291456]{0:T(1024)(128)(4,1)} %bitcast.89), calls=%async_computation.7 | async-start | bytes 8388608
  769.3 8.5 %slice-start.3 = ((s8[6291456]{0:T(1024)(128)(4,1)}), s8[2097152]{0:T(1024)(128)(4,1)S(1)}, s32[]{:S(2)}) async-start(s8[6291456]{0:T(1024)(128)(4,1)} %bitcast.89), calls=%async_computation.8 | async-start | bytes 4194304
  788.2 2.4 copy-start.1
  790.6 6.3 copy-start.2
  790.6 11.7 %slice-start = ((s8[6291456]{0:T(1024)(128)(4,1)}), s8[4194304]{0:T(1024)(128)(4,1)S(1)}, s32[]{:S(2)}) async-start(s8[6291456]{0:T(1024)(128)(4,1)} %bitcast.82), calls=%async_computation.5 | async-start | bytes 8388608
  795.4 6.9 slice-start.1
Sparse Core Ops, SparseCore 0:
  10.9 64.4 all-gather.7
  77.5 35.8 all-gather.13
  115.5 35.8 all-gather.11
  153.2 26.6 all-gather.9
  181.6 27.7 all-gather.5
where the time goes:
time: 822 us; the launch traced here: 817 us
  other arithmetic  528 us (64%)
  waiting for transfers between devices  155 us (19%)
  matrix products  114 us (14%)
  between operations  14.3 us (2%)
    another operation x7, other arithmetic, small_inverse(): factor = jnp.linalg.cholesky(gram_matrix)  283 us
    another operation x5, other arithmetic, small_inverse(): return jax.scipy.linalg.solve_triangular(factor, eye_block, lower=True)  237 us
    all_gather x1, waiting for transfers between devices, body(): lax.all_gather(diag_inverse, ('row', 'col'), axis=0, tiled=True)  64.7 us
    all_gather x1, waiting for transfers between devices, body(): lax.all_gather(col_send, 'row', axis=1, tiled=True)  31.3 us
    all_gather x1, waiting for transfers between devices, body(): lax.all_gather(row_send, 'col', axis=1, tiled=True)  28.4 us
    all_gather x1, waiting for transfers between devices, body(): lax.all_gather(row_left, 'col', axis=1, tiled=True)  23.1 us
  transfers between devices with their start and end apart: 5, of which 5 were waited for; matrix products, arithmetic and copies ran while one was open for 6% of the time, Pallas kernels for 0%

commit v1 on v0

--- a/solution.py
+++ b/solution.py
@@ -3,29 +3,108 @@
 import jax
 import jax.numpy as jnp
 from jax import lax
+from jax.experimental import pallas as pl
+from jax.experimental.pallas import tpu as pltpu
 from jax.sharding import PartitionSpec as P
 
 HIGHEST = lax.Precision.HIGHEST
 
 
-def small_inverse(gram_matrix, eye_block):
-    factor = jnp.linalg.cholesky(gram_matrix)
-    return jax.scipy.linalg.solve_triangular(factor, eye_block, lower=True)
+HIGH = lax.Precision.HIGH
+PIVOT_ROWS = 32
+
+
+def batch_dot(left, right, left_dim, right_dim):
+    dims = (((left_dim,), (right_dim,)), ((), ()))
+    return lax.dot_general(
+        left, right, dims, precision=HIGHEST, preferred_element_type=jnp.float32
+    )
+
+
+def factor_inverse_into(work_ref, tile_count, width):
+    rows = PIVOT_ROWS
+    lane_half = width // 2
+    row_ids = lax.broadcasted_iota(jnp.int32, (1, rows, 1), 1)
+    eye_lane = (
+        lax.broadcasted_iota(jnp.int32, (1, rows, width), 1)
+        == lax.broadcasted_iota(jnp.int32, (1, rows, width), 2)
+    ).astype(jnp.float32)
+    pick_row = lax.broadcasted_iota(jnp.int32, (width, width), 0)
+    pick_lane = lax.broadcasted_iota(jnp.int32, (width, width), 1)
+    lane_ids = lax.broadcasted_iota(jnp.int32, (rows, width), 1)
+
+    def block_step(block, carry):
+        start = pl.multiple_of(block * rows, rows)
+        picker = jnp.where(
+            (pick_lane >= lane_half)
+            & (pick_lane < lane_half + rows)
+            & (pick_row == start + pick_lane - lane_half),
+            1.0,
+            0.0,
+        )
+        strip = work_ref[:, pl.ds(start, rows), :width].reshape(tile_count * rows, width)
+        state = batch_dot(strip, picker, 1, 0).reshape(tile_count, rows, width) + eye_lane
+        pivots = jnp.zeros((tile_count, rows, 1), jnp.float32)
+        for j in range(rows):
+            column = state[:, :, lane_half + j : lane_half + j + 1]
+            pivot = column[:, j : j + 1, :]
+            pivots = jnp.where(row_ids == j, pivot, pivots)
+            if j < rows - 1:
+                multiplier = jnp.where(row_ids > j, column / pivot, 0.0)
+                state = state - multiplier * state[:, j : j + 1, :]
+        state = state * (1.0 / jnp.sqrt(pivots))
+        for t in range(tile_count):
+            solved = batch_dot(state[t, :, :rows], work_ref[t, pl.ds(start, rows), :], 1, 0)
+            below = jnp.where(lane_ids >= start + rows, solved[:, :width], 0.0)
+            work_ref[t] = work_ref[t] - batch_dot(below, solved, 0, 0)
+            work_ref[t, pl.ds(start, rows), :] = solved
+        return carry
+
+    lax.fori_loop(0, width // rows, block_step, 0)
+
+
+def twice_kernel(gram_ref, out_ref, work_ref):
+    tile_count, width, _ = gram_ref.shape
+    eye = (
+        lax.broadcasted_iota(jnp.int32, (width, width), 0)
+        == lax.broadcasted_iota(jnp.int32, (width, width), 1)
+    ).astype(jnp.float32)
+    for t in range(tile_count):
+        out_ref[t] = eye
+
+    def one_pass(step, carry):
+        for t in range(tile_count):
+            inverse = out_ref[t]
+            again = batch_dot(inverse, batch_dot(gram_ref[t], inverse, 1, 1), 1, 0)
+            work_ref[t, :, :width] = 0.5 * (again + again.T)
+            work_ref[t, :, width:] = eye
+        factor_inverse_into(work_ref, tile_count, width)
+        for t in range(tile_count):
+            out_ref[t] = batch_dot(work_ref[t, :, width:], out_ref[t], 1, 0)
+        return carry
+
+    lax.fori_loop(0, 2, one_pass, 0)
+
+
+def combined_inverse(gram_matrix):
+    tile_count, width, _ = gram_matrix.shape
+    return pl.pallas_call(
+        twice_kernel,
+        out_shape=jax.ShapeDtypeStruct(gram_matrix.shape, jnp.float32),
+        in_specs=[pl.BlockSpec(memory_space=pltpu.VMEM)],
+        out_specs=pl.BlockSpec(memory_space=pltpu.VMEM),
+        scratch_shapes=[pltpu.VMEM((tile_count, width, 2 * width), jnp.float32)],
+        name="factor_twice",
+    )(gram_matrix)
 
 
 def orthonormal_twice(sketch_block, rank_keep):
     rank_width = rank_keep.shape[-1]
     eye_one = jnp.eye(rank_width, dtype=jnp.float32)[None, :, :]
-    eye_block = jnp.broadcast_to(eye_one, (sketch_block.shape[0], rank_width, rank_width))
     gram_matrix = jnp.einsum("tnr,tns->trs", sketch_block, sketch_block, precision=HIGHEST)
     gram_matrix = gram_matrix + eye_one * (1.0 - rank_keep)[:, None, :]
-    first_inverse = small_inverse(gram_matrix, eye_block)
-    half_gram = jnp.einsum("trs,tus->tru", gram_matrix, first_inverse, precision=HIGHEST)
-    second_gram = jnp.einsum("trs,tsu->tru", first_inverse, half_gram, precision=HIGHEST)
-    second_gram = 0.5 * (second_gram + jnp.swapaxes(second_gram, 1, 2))
-    second_inverse = small_inverse(second_gram, eye_block)
-    combined = jnp.einsum("trs,tsu->tru", second_inverse, first_inverse, precision=HIGHEST)
-    return jnp.einsum("tnr,tsr->tns", sketch_block, combined, precision=HIGHEST)
+    combined = combined_inverse(gram_matrix)
+    return jnp.einsum("tnr,tsr->tns", sketch_block, combined, precision=HIGH)
 
 
 def share_mask(panel_ranks, rank_share, position):
@@ -73,7 +152,7 @@
     all_coupling = jnp.dot(
         row_solved.reshape(local_rows * rank_width, order),
         col_solved.reshape(local_cols * rank_width, order).T,
-        precision=HIGHEST,
+        precision=HIGH,
     )
     coupling = jnp.transpose(
         all_coupling.reshape(local_rows, rank_width, local_cols, rank_width), (0, 2, 1, 3)
@@ -86,10 +165,10 @@
     masked_right = tile_coef * rank_keep[:, :, None, :]
 
     def make_sketch(tile_left, tile_right, left_panel, pair_coupling, right_panel):
-        inner_gram = jnp.dot(tile_right.T, tile_right, precision=HIGHEST)
-        cross_term = jnp.dot(right_panel, tile_right, precision=HIGHEST)
-        return jnp.dot(tile_left, inner_gram, precision=HIGHEST) - jnp.dot(
-            left_panel.T, jnp.dot(pair_coupling, cross_term, precision=HIGHEST), precision=HIGHEST
+        inner_gram = jnp.dot(tile_right.T, tile_right, precision=HIGH)
+        cross_term = jnp.dot(right_panel, tile_right, precision=HIGH)
+        return jnp.dot(tile_left, inner_gram, precision=HIGH) - jnp.dot(
+            left_panel.T, jnp.dot(pair_coupling, cross_term, precision=HIGH), precision=HIGH
         )
 
     sketch_inner = jax.vmap(make_sketch, in_axes=(0, 0, None, 0, 0))
@@ -104,11 +183,11 @@
 
     def make_coef(tile_left, tile_right, left_panel, pair_coupling, right_panel, basis_block):
         first_part = jnp.dot(
-            tile_right, jnp.dot(tile_left.T, basis_block, precision=HIGHEST), precision=HIGHEST
-        )
-        left_proj = jnp.dot(left_panel, basis_block, precision=HIGHEST)
+            tile_right, jnp.dot(tile_left.T, basis_block, precision=HIGH), precision=HIGH
+        )
+        left_proj = jnp.dot(left_panel, basis_block, precision=HIGH)
         second_part = jnp.dot(
-            right_panel.T, jnp.dot(pair_coupling.T, left_proj, precision=HIGHEST), precision=HIGHEST
+            right_panel.T, jnp.dot(pair_coupling.T, left_proj, precision=HIGH), precision=HIGH
         )
         return first_part - second_part
 

time: 822 us -> 407 us (0.50)
  other arithmetic: 528 us -> 5.94 us
  Pallas kernels: 0 us -> 137 us
  matrix products: 114 us -> 77.5 us
    another operation x12 -> x0, other arithmetic: 520 us -> none  [the longest x7 283 us: small_inverse(): factor = jnp.linalg.cholesky(gram_matrix)]
    pallas_call x0 -> x1, Pallas kernels: none -> 137 us  [combined_inverse(): pl.pallas_call(twice_kernel, out_shape=jax.ShapeDtypeStruct(gram_matrix.s...]
    dot_general x13 -> x10, matrix products: 74.6 us -> 45.3 us  [the longest x1 9.73 us: make_sketch(): inner_gram = jnp.dot(tile_right.T, tile_right, precision=HIGH)]
  transfers between devices with their start and end apart: 5 -> 5, of which waited for: 5 -> 5; matrix products, arithmetic and copies ran while one was open for 6% -> 10% of each run, Pallas kernels for 0% -> 0%
where the time goes in v1:
time: 407 us; the launch traced here: 401 us
  waiting for transfers between devices  163 us (40%)
  Pallas kernels  137 us (34%)
  matrix products  77.5 us (19%)
  between operations  14.2 us (3%)
  other arithmetic  5.94 us (1%)
    pallas_call x1, Pallas kernels, combined_inverse(): pl.pallas_call(twice_kernel, out_shape=jax.ShapeDtypeStruct(gram_matrix.s...  137 us
    all_gather x1, waiting for transfers between devices, body(): lax.all_gather(diag_inverse, ('row', 'col'), axis=0, tiled=True)  64.7 us
    all_gather x1, waiting for transfers between devices, body(): lax.all_gather(col_send, 'row', axis=1, tiled=True)  32.8 us
    all_gather x1, waiting for transfers between devices, body(): lax.all_gather(row_send, 'col', axis=1, tiled=True)  28.4 us
    all_gather x1, waiting for transfers between devices, body(): lax.all_gather(row_left, 'col', axis=1, tiled=True)  24.4 us
    dot_general x2, matrix products, solve_rows(): solved = jnp.dot(flat_rows, inverse_factor.T, precision=HIGHEST)  14.4 us
    all_gather x1, waiting for transfers between devices, body(): lax.all_gather(col_left, 'row', axis=1, tiled=True)  12.4 us
    dot_general x1, matrix products, orthonormal_twice(): jnp.einsum('tnr,tns->trs', sketch_block, sketch_block, precision=HIGHEST)  11.3 us
  transfers between devices with their start and end apart: 5, of which 5 were waited for; matrix products, arithmetic and copies ran while one was open for 10% of the time, Pallas kernels for 0%

profile of v1, /device:TPU:0, one launch (start us, length us, event | category | flops | bytes accessed | tf_op | source)
XLA Modules:
  0.0 401.5 jit_solution(10384469984824329578)
XLA Ops:
  8.7 1.8 broadcast_multiply_fusion.1
  10.6 64.7 %all-gather.8.cloned.1.call-done = f32[1024,1024]{1,0:T(8,128)} async-done(((f32[32,1024]{1,0:T(8,128)}), f32[1024,1024]{1,0:T(8,128)}) %all-gather.8.cloned.1.call-update) | async-done | bytes 4194320 | tf_op jit(solution)/shard_map/all_gather | solution.py:134
  75.4 7.2 %fusion.7 = f32[3,32,1024]{2,1,0:T(8,128)} fusion(f32[1024,1024]{1,0:T(8,128)} %all-gather.8.cloned.1.call-done, f32[3,32,1024]{2,1,0:T(8,128)} %param.15, f32[3,32]{1,0:T(4,128)S(1)} %compare_convert_fusion), kind=kOutput, calls=%fused_computation.10 | convolution fusion | flops 1208057856 | bytes 4981120 | tf_op jit(solution)/shard_map/dot_general | solution.py:118
  82.7 7.2 %fusion.9 = f32[4,16,1024]{2,1,0:T(8,128)} fusion(f32[1024,1024]{1,0:T(8,128)} %all-gather.8.cloned.1.call-done, f32[4,16,1024]{2,1,0:T(8,128)S(1)} %copy-done.3, f32[4,16]{1,0:T(4,128)S(1)} %compare_convert_fusion.1), kind=kOutput, calls=%fused_computation.12 | convolution fusion | flops 805371904 | bytes 4718848 | tf_op jit(solution)/shard_map/dot_general | solution.py:118
  91.2 9.7 %fusion.38 = f32[4,3,128,128]{3,2,1,0:T(8,128)S(1)} fusion(f32[4,3,1024,128]{3,2,1,0:T(8,128)} %param.18, f32[4,3,128]{2,1,0:T(4,128)S(1)} %fusion.37), kind=kOutput, calls=%fused_computation.51 | convolution fusion | flops 1211105280 | bytes 7084032 | tf_op jit(solution)/shard_map/vmap(vmap())/dot_general | solution.py:168
  101.0 12.4 %all-gather.14.cloned.1.call-done = f32[3,128,1024]{2,1,0:T(8,128)} async-done(((f32[3,32,1024]{2,1,0:T(8,128)}), f32[3,128,1024]{2,1,0:T(8,128)}) %all-gather.14.cloned.1.call-update) | async-done | bytes 1572880 | tf_op jit(solution)/shard_map/all_gather | solution.py:148
  113.4 5.2 %fusion.1 = f32[3,128,4,128]{3,1,2,0:T(8,128)S(1)} fusion(f32[3,128,1024]{2,1,0:T(8,128)} %all-gather.14.cloned.1.call-done, f32[4,3,1024,128]{3,2,1,0:T(8,128)} %param.18, f32[4,3,128]{2,1,0:T(4,128)S(1)} %fusion.37), kind=kOutput, calls=%fused_computation.3 | convolution fusion | flops 1209532416 | bytes 8656896 | tf_op jit(solution)/shard_map/vmap(vmap())/dot_general | solution.py:169
  118.6 32.8 %all-gather.12.cloned.1.call-done = f32[3,128,1024]{2,1,0:T(8,128)} async-done(((f32[3,32,1024]{2,1,0:T(8,128)}), f32[3,128,1024]{2,1,0:T(8,128)}) %all-gather.12.cloned.1.call-update) | async-done | bytes 1572880 | tf_op jit(solution)/shard_map/all_gather | solution.py:149
  151.4 28.4 %all-gather.10.cloned.1.call-done = f32[4,128,1024]{2,1,0:T(8,128)} async-done(((f32[4,16,1024]{2,1,0:T(8,128)}), f32[4,128,1024]{2,1,0:T(8,128)}) %all-gather.10.cloned.1.call-update) | async-done | bytes 2097168 | tf_op jit(solution)/shard_map/all_gather | solution.py:141
  179.8 3.8 fusion.15
  183.7 1.4 fusion.27
  185.1 24.4 %all-gather.6.cloned.1.call-done = f32[4,128,1024]{2,1,0:T(8,128)} async-done(((f32[4,16,1024]{2,1,0:T(8,128)}), f32[4,128,1024]{2,1,0:T(8,128)}) %all-gather.6.cloned.1.call-update) | async-done | bytes 2097168 | tf_op jit(solution)/shard_map/all_gather | solution.py:140
  209.4 5.0 %fusion.19 = f32[4,1024,3,128]{3,1,2,0:T(8,128)S(1)} fusion(f32[4,3,128,128]{3,2,1,0:T(8,128)} %fusion.27, f32[4,128,1024]{2,1,0:T(8,128)} %all-gather.6.cloned.1.call-done), kind=kOutput, calls=%fused_computation.21 | convolution fusion | flops 1207959552 | bytes 9175040 | tf_op jit(solution)/shard_map/vmap(vmap())/dot_general | solution.py:170
  214.4 5.0 %bitcast_subtract_fusion.1 = f32[4,3,1024,128]{3,2,1,0:T(8,128)S(1)} fusion(f32[4,1024,3,128]{3,1,2,0:T(8,128)S(1)} %fusion.19, f32[4,3,128,128]{3,2,1,0:T(8,128)S(1)} %fusion.38, f32[4,3,1024,128]{3,2,1,0:T(8,128)} %param.17, f32[4,3,128]{2,1,0:T(4,128)S(1)} %fusion.37), kind=kOutput, calls=%fused_computation.2 | convolution fusion | flops 1211105280 | bytes 19666944 | tf_op jit(solution)/shard_map/vmap(vmap())/dot_general | solution.py:170
  219.4 2.6 copy-done
  222.1 11.3 %convolution_add_fusion.gram_ref = f32[12,128,128]{2,1,0:T(8,128)} fusion(f32[12,1024,128]{2,1,0:T(8,128)S(1)} %bitcast.56, f32[12,128]{1,0:T(8,128)S(1)} %convert_subtract_fusion, f32[128,128]{1,0:T(8,128)S(1)} %fusion.36), kind=kOutput, calls=%fused_computation.27 | convolution fusion | flops 2416312320 | bytes 7149568 | tf_op jit(solution)/shard_map/tnr,tns->trs/dot_general | solution.py:104
  233.3 137.2 %factor_twice.1 = f32[12,128,128]{2,1,0:T(8,128)} custom-call(f32[12,128,128]{2,1,0:T(8,128)} %convolution_add_fusion.gram_ref), custom_call_target="tpu_custom_call" | custom-call | tf_op jit(solution)/shard_map/factor_twice/pallas_call | solution.py:91
  370.5 5.5 %fusion.39 = f32[12,1024,128]{2,1,0:T(8,128)S(1)} fusion(f32[12,1024,128]{2,1,0:T(8,128)} %bitcast.57, f32[12,128,128]{2,1,0:T(8,128)} %factor_twice.1), kind=kOutput, calls=%fused_computation.52 | convolution fusion | flops 1207959552 | bytes 13369344 | tf_op jit(solution)/shard_map/tnr,tsr->tns/dot_general | solution.py:107
  376.1 5.5 %fusion.3 = f32[4,3,128,128]{3,2,1,0:T(8,128)S(1)} fusion(f32[4,3,1024,128]{3,2,1,0:T(8,128)S(1)} %bitcast.58, f32[4,3,1024,128]{3,2,1,0:T(8,128)S(1)} %bitcast.62, f32[4,3,128]{2,1,0:T(4,128)S(1)} %fusion.37), kind=kOutput, calls=%fused_computation.6 | convolution fusion | flops 1209532416 | bytes 13375488 | tf_op jit(solution)/shard_map/vmap(vmap())/dot_general | solution.py:186
  381.6 2.4 multiply_convert_fusion
  383.9 2.6 fusion.17
  386.5 0.8 fusion.25
  387.4 2.7 fusion.22
  390.1 4.6 %fusion = bf16[4,3,1024,128]{3,2,1,0:T(8,128)(2,1)} fusion(f32[3,1024,4,128]{3,1,0,2:T(8,128)S(1)} %fusion.22, f32[4,3,128,128]{3,2,1,0:T(8,128)S(1)} %fusion.3, f32[4,3,1024,128]{3,2,1,0:T(8,128)S(1)} %bitcast.55, f32[4,3,128]{2,1,0:T(4,128)S(1)} %fusion.37), kind=kOutput, calls=%fused_computation.1 | convolution fusion | flops 1212678144 | bytes 16521216 | tf_op jit(solution)/shard_map/vmap(vmap())/dot_general | solution.py:185
  (42 shorter events, 3.0 us)
Async XLA Ops:
  7.2 75.5 %copy-start.6 = (s32[4]{0:T(128)S(1)}, s32[4]{0:T(128)}, u32[]{:S(2)}) copy-start(s32[4]{0:T(128)} %param.13) | copy-start | bytes 52
  7.2 75.6 %copy-start.3 = (f32[4,16,1024]{2,1,0:T(8,128)S(1)}, f32[4,16,1024]{2,1,0:T(8,128)}, u32[]{:S(2)}) copy-start(f32[4,16,1024]{2,1,0:T(8,128)} %param.12) | copy-start | bytes 786436
  7.2 83.0 %copy-start.4 = (f32[4,16,1024]{2,1,0:T(8,128)S(1)}, f32[4,16,1024]{2,1,0:T(8,128)}, u32[]{:S(2)}) copy-start(f32[4,16,1024]{2,1,0:T(8,128)} %param.11) | copy-start | bytes 786436
  7.2 83.8 %copy-start.5 = (s32[4,3]{1,0:T(4,128)S(1)}, s32[4,3]{1,0:T(4,128)}, u32[]{:S(2)}) copy-start(s32[4,3]{1,0:T(4,128)} %param.19) | copy-start | bytes 148
  7.2 68.1 %all-gather.8.cloned.1.call-start = ((), (), s32[]{:S(2)}) async-start(), calls=%async_computation.1 | async-start | bytes 4325376 | tf_op jit(solution)/shard_map/all_gather | solution.py:134
  7.9 105.4 %all-gather.14.cloned.1.call-start = ((), (), s32[]{:S(2)}) async-start(), calls=%async_computation.4 | async-start | bytes 1966080 | tf_op jit(solution)/shard_map/all_gather | solution.py:148
  10.6 140.8 %all-gather.12.cloned.1.call-start = ((), (), s32[]{:S(2)}) async-start(), calls=%async_computation.3 | async-start | bytes 1966080 | tf_op jit(solution)/shard_map/all_gather | solution.py:149
  82.6 97.3 %all-gather.10.cloned.1.call-start = ((), (), s32[]{:S(2)}) async-start(), calls=%async_computation.2 | async-start | bytes 2359296 | tf_op jit(solution)/shard_map/all_gather | solution.py:141
  89.9 119.5 %all-gather.6.cloned.1.call-start = ((), (), s32[]{:S(2)}) async-start(), calls=%async_computation | async-start | bytes 2359296 | tf_op jit(solution)/shard_map/all_gather | solution.py:140
  219.4 2.6 copy-start
  233.3 142.7 %slice-start.2 = ((s8[6291456]{0:T(1024)(128)(4,1)}), s8[2097152]{0:T(1024)(128)(4,1)S(1)}, s32[]{:S(2)}) async-start(s8[6291456]{0:T(1024)(128)(4,1)} %bitcast.61), calls=%async_computation.7 | async-start | bytes 4194304
  370.5 5.5 %slice-start.3 = ((s8[6291456]{0:T(1024)(128)(4,1)}), s8[4194304]{0:T(1024)(128)(4,1)S(1)}, s32[]{:S(2)}) async-start(s8[6291456]{0:T(1024)(128)(4,1)} %bitcast.61), calls=%async_computation.8 | async-start | bytes 8388608
  381.5 2.4 copy-start.1
  383.9 3.4 copy-start.2
  383.9 6.2 %slice-start = ((s8[6291456]{0:T(1024)(128)(4,1)}), s8[4194304]{0:T(1024)(128)(4,1)S(1)}, s32[]{:S(2)}) async-start(s8[6291456]{0:T(1024)(128)(4,1)} %bitcast.54), calls=%async_computation.5 | async-start | bytes 8388608
  386.5 3.6 slice-start.1
Sparse Core Ops, SparseCore 0:
  10.9 64.4 all-gather.7
  77.5 35.8 all-gather.13
  115.5 35.8 all-gather.11
  153.2 26.6 all-gather.9
  181.6 27.7 all-gather.5
